TPU v7x, 32 devices: a whole 2x2x4 slice. The times are simulated.
32 devices in a mesh: group: 2 (over y), tile: 8 (over z, x), strip: 2 (over core).
Axes of the slice: x: 2, y: 2, z: 4, core: 2. Of those that a mesh axis runs over, the one named last changes fastest.
Arguments:
- image: bfloat16 [128, 256, 256], P(('group', 'strip'), 'tile'), parts along dimension 0, may hold values from -16 to 16
- bn_gain: float32 [256], replicated, may hold values from 0.25 to 1.75
- bn_shift: float32 [256], replicated, may hold values from -3 to 3
- w_expand: bfloat16 [256, 1024], replicated, may hold values from -0.375 to 0.375
- b_expand: float32 [1024], replicated, may hold values from -3 to 3
- w_depth: float32 [9, 1024], replicated, may hold values from -2 to 2
- b_depth: float32 [1024], replicated, may hold values from -3 to 3
- w_project: bfloat16 [1024, 256], replicated, may hold values from -0.1875 to 0.1875
- b_project: float32 [256], replicated, may hold values from -3 to 3
- attn_gain: float32 [256], replicated, may hold values from 0.25 to 1.75
- attn_shift: float32 [256], replicated, may hold values from -2 to 2
- w_qkv: bfloat16 [256, 768], replicated, may hold values from -0.375 to 0.375
- w_out: bfloat16 [256, 256], replicated, may hold values from -0.375 to 0.375
- rel_table: float32 [8, 225], replicated, may hold values from -4 to 304
- ffn_gain: float32 [256], replicated, may hold values from 0.25 to 1.75
- ffn_shift: float32 [256], replicated, may hold values from -2 to 2
- w_up: bfloat16 [256, 1024], replicated, may hold values from -0.375 to 0.375
- b_up: float32 [1024], replicated, may hold values from -3 to 3
- w_down: bfloat16 [1024, 256], replicated, may hold values from -0.1875 to 0.1875
- b_down: float32 [256], replicated, may hold values from -3 to 3
Outputs:
- block_out: bfloat16 [128, 256, 256], P(('group', 'strip'), 'tile'), parts along dimension 0
There are 2 independent parts, one for each index of `group`. A program takes and returns all parts, laid end to end along the dimension named above; an argument that names none is the same for every part. Nothing has to cross between parts.
All inputs are finite; a program needn't handle non-finite values.
Results may differ from a plain program's by a relative error of at most 0.0064.
Values may be sent and summed in bfloat16 or wider, within the bound.
A program may use at most 64 MiB of HBM per device.

v0:
```python
import functools

import jax
import jax.numpy as jnp
from jax import lax
from jax.experimental import pallas as pl
from jax.experimental.pallas import tpu as pltpu
from jax.sharding import PartitionSpec as P

GRID = 8
EPSILON = 1e-05
MESH = pl.DeviceIdType.MESH


def gelu_tanh(inputs):
    return jax.nn.gelu(inputs, approximate=True)


def layer_norm(inputs, norm_gain, norm_shift):
    center = jnp.mean(inputs, axis=-1, keepdims=True)
    spread = jnp.mean(jnp.square(inputs - center), axis=-1, keepdims=True)
    return (inputs - center) * lax.rsqrt(spread + EPSILON) * norm_gain + norm_shift


def place_bias(rel_table):
    heads = rel_table.shape[0]
    side = 2 * GRID - 1
    table = rel_table.reshape(heads, side, side)
    shape = (side, GRID, GRID)
    entry = lax.broadcasted_iota(jnp.int32, shape, 0)
    key = lax.broadcasted_iota(jnp.int32, shape, 1)
    query = lax.broadcasted_iota(jnp.int32, shape, 2)
    onehot = (entry == GRID - 1 + query - key).astype(jnp.float32)
    by_col = jnp.einsum("hde,eki->dkhi", table, onehot, precision=lax.Precision.HIGHEST)
    by_col = by_col.reshape(side, GRID, heads * GRID)
    return jnp.concatenate([by_col[:-1], by_col[1:]], axis=-1)


def dot(a, b):
    return jnp.dot(a, b, preferred_element_type=jnp.float32)


def block_kernel(
    strips,
    col_groups,
    head_count,
    image_ref,
    bng_ref,
    bns_ref,
    wexp_ref,
    bexp_ref,
    wdep_ref,
    bdep_ref,
    wproj_ref,
    bproj_ref,
    ag_ref,
    as_ref,
    wqkv_ref,
    wout_ref,
    bias_ref,
    fg_ref,
    fs_ref,
    wup_ref,
    bup_ref,
    wdown_ref,
    bdown_ref,
    out_ref,
    edge,
    cols_in,
    rows_in,
    rim,
    e_s,
    h_s,
    sec_ref,
    arr,
    q_s,
    k_s,
    v_s,
    ctx_s,
    outb,
    sec2,
    send1,
    recv1,
    send2,
    recv2,
    hsend,
    hrecv,
):
    grid_rows, _, cols, chans = sec_ref.shape
    part = cols // strips
    rows = image_ref.shape[0]
    piece = ctx_s.shape[1]
    blocks = GRID * GRID // piece
    per_block = piece // GRID
    head_size = chans // head_count
    me_s = lax.axis_index("strip")
    tile = lax.axis_index("tile")
    me_k = tile // col_groups
    within = tile % col_groups
    peers = strips * GRID

    def device(s, k):
        return {"strip": s, "tile": k * col_groups + within}

    def is_me(s, k):
        return jnp.logical_and(s == me_s, k == me_k)

    barrier = pltpu.get_barrier_semaphore()
    for m in range(1, peers):
        s, k = (me_s + m // GRID) % strips, (me_k + m) % GRID
        pl.semaphore_signal(barrier, inc=1, device_id=device(s, k), device_id_type=MESH)
    tiles = GRID * col_groups
    sides = ((tile + tiles - 1) % tiles, (tile + 1) % tiles)
    for t in sides:
        for s in range(strips):
            pl.semaphore_signal(
                barrier, inc=1, device_id={"strip": s, "tile": t}, device_id_type=MESH
            )
    pl.semaphore_wait(barrier, peers - 1 + 2 * strips)

    edge[0] = image_ref[:, 0:16, :].astype(jnp.float32)[:, 0, :].astype(jnp.bfloat16)
    edge[1] = image_ref[:, cols - 16 : cols, :].astype(jnp.float32)[:, 15, :].astype(jnp.bfloat16)
    halo = []
    for i in range(2):
        for s in range(strips):
            halo.append(
                pltpu.make_async_remote_copy(
                    edge.at[i],
                    cols_in.at[1 - i, me_s],
                    hsend.at[i, s],
                    hrecv.at[1 - i, me_s],
                    device_id={"strip": s, "tile": sides[i]},
                    device_id_type=MESH,
                )
            )
    for i in range(2):
        halo.append(
            pltpu.make_async_remote_copy(
                image_ref.at[(rows - 1) * (1 - i)],
                rows_in.at[i],
                hsend.at[2, i],
                hrecv.at[2, i],
                device_id={"strip": (me_s + 1 + i * (strips - 2)) % strips, "tile": tile},
                device_id_type=MESH,
            )
        )
    for copy in halo:
        copy.start()

    lanes = 128
    chunks = wexp_ref.shape[1] // lanes
    pad = 8
    group = 4

    def expand(pixels):
        normed = (pixels.astype(jnp.float32) * bng_ref[...] + bns_ref[...]).astype(jnp.bfloat16)
        return gelu_tanh(dot(normed, wexp_ref[...]) + bexp_ref[...])

    @pl.loop(0, rows // group)
    def _(q):
        pixels = image_ref[pl.ds(group * q, group)].reshape(group * cols, chans)
        act = expand(pixels)
        for c in range(chunks):
            e_s[pl.ds(group * q + 1, group), c, pad : pad + cols, :] = act[
                :, lanes * c : lanes * (c + 1)
            ].reshape(group, cols, lanes)

    for i in range(2):
        for s in range(strips):
            pltpu.make_async_copy(cols_in.at[i, s], cols_in.at[i, s], hrecv.at[i, s]).wait()
        pltpu.make_async_copy(rows_in.at[i], rows_in.at[i], hrecv.at[2, i]).wait()
    row_ok = (
        jnp.where(me_s > 0, 1.0, 0.0),
        jnp.where(me_s < strips - 1, 1.0, 0.0),
    )
    col_ok = (
        jnp.where(tile > 0, 1.0, 0.0),
        jnp.where(tile < tiles - 1, 1.0, 0.0),
    )
    for i in range(2):
        act = expand(rows_in[i]) * row_ok[i]
        for c in range(chunks):
            e_s[(rows + 1) * i, c, pad : pad + cols, :] = act[:, lanes * c : lanes * (c + 1)]
        act = expand(cols_in[i].reshape(strips * rows, chans)) * col_ok[i]
        rim[i, 0:8] = jnp.zeros((8, act.shape[1]), jnp.float32)
        rim[i, 8 : 8 + strips * rows] = act
        rim[i, 8 + strips * rows :] = jnp.zeros((8, act.shape[1]), jnp.float32)

    for i in range(2):
        at = (pad + cols) * i

        @pl.loop(0, rows + 2)
        def _(r):
            line = rim[i, pl.ds(me_s * rows + 7 + r, 1), :]
            for c in range(chunks):
                e_s[r, c, at : at + 8, :] = jnp.broadcast_to(
                    line[:, lanes * c : lanes * (c + 1)], (8, lanes)
                )

    def first_copy(s, k, g):
        src = sec_ref.at[g, k, pl.ds(part * s, part)]
        dst = arr.at[grid_rows * me_s + g, me_k]
        return (
            lambda: pltpu.make_async_remote_copy(
                src,
                dst,
                send1.at[s, k],
                recv1.at[me_s, me_k],
                device_id=device(s, k),
                device_id_type=MESH,
            ),
            lambda: pltpu.make_async_copy(src, dst, recv1.at[me_s, me_k]),
        )

    groups = rows // group
    per_grid = groups // grid_rows
    far = (me_k // (GRID // per_grid) + 1) % per_grid

    @pl.loop(0, groups)
    def _(m):
        g = m % grid_rows
        sub = (far + m // grid_rows) % per_grid
        q = per_grid * g + sub
        for c in range(chunks):
            at = slice(lanes * c, lanes * (c + 1))
            acc = [jnp.broadcast_to(bdep_ref[:, at], (cols, lanes))] * group
            for r in range(group + 2):
                for j in range(3):
                    v = e_s[group * q + r, c, pad - 1 + j : pad - 1 + j + cols, :]
                    for o in range(group):
                        if 0 <= r - o <= 2:
                            tap = 3 * (r - o) + j
                            acc[o] = acc[o] + v * wdep_ref[tap : tap + 1, at]
            for o in range(group):
                h_s[cols * o : cols * (o + 1), at] = gelu_tanh(acc[o]).astype(jnp.bfloat16)
        skip = image_ref[pl.ds(group * q, group)].reshape(group * cols, chans).astype(jnp.float32)
        sec = skip + dot(h_s[...], wproj_ref[...]) + bproj_ref[...]
        sec_ref[g, pl.ds(group * sub, group)] = sec.astype(jnp.bfloat16).reshape(
            group, cols, chans
        )
        for r in range(group):
            for s in range(strips):
                k = group * sub + r
                remote, own = first_copy(s, k, g)

                @pl.when(jnp.logical_not(is_me(s, k)))
                def _():
                    remote().start()

                @pl.when(is_me(s, k))
                def _():
                    own().start()

    def wait_first(s, k):
        piece_ref = arr.at[pl.ds(grid_rows * s, grid_rows), k]
        pltpu.make_async_copy(piece_ref, piece_ref, recv1.at[s, k]).wait()

    span = piece * part
    row_id = lax.broadcasted_iota(jnp.int32, (span, span), 0)
    col_id = lax.broadcasted_iota(jnp.int32, (span, span), 1)
    swap = jnp.where(col_id == (row_id % piece) * part + row_id // piece, 1.0, 0.0).astype(
        jnp.bfloat16
    )
    lane_head = lax.broadcasted_iota(jnp.int32, (head_count * piece, chans), 1) // head_size
    row_id = lax.broadcasted_iota(jnp.int32, (head_count * piece, chans), 0)
    row_head = row_id // GRID % head_count
    mask = jnp.where(lane_head == row_head, 1.0, 0.0)
    mask_bf = mask.astype(jnp.bfloat16)

    blocks_per_strip = blocks // strips
    for b in range(blocks):
        if b % blocks_per_strip == 0:
            for k in range(GRID):
                wait_first(b // blocks_per_strip, k)
        x = arr[per_block * b : per_block * (b + 1)].reshape(span, chans).astype(jnp.float32)
        normed = layer_norm(x, ag_ref[...], as_ref[...]).astype(jnp.bfloat16)
        normed = dot(swap, normed).astype(jnp.bfloat16)
        qkv = dot(normed, wqkv_ref[...])
        q = (qkv[:, :chans] * head_size ** (-0.5)).reshape(part, per_block, GRID, chans)
        q_s[b] = jnp.concatenate([q, q], axis=2).astype(jnp.bfloat16)
        k_s[:, piece * b : piece * (b + 1), :] = (
            qkv[:, chans : 2 * chans].astype(jnp.bfloat16).reshape(part, piece, chans)
        )
        v_s[:, piece * b : piece * (b + 1), :] = (
            qkv[:, 2 * chans :].astype(jnp.bfloat16).reshape(part, piece, chans)
        )

    def back_copy(b, k):
        s = b // blocks_per_strip
        half = b % blocks_per_strip
        src = outb.at[pl.ds(per_block * b, per_block), k]
        dst = sec2.at[pl.ds(per_block * half, per_block), me_k, pl.ds(part * me_s, part)]
        return (
            s,
            lambda: pltpu.make_async_remote_copy(
                src,
                dst,
                send2.at[b, k],
                recv2.at[half, me_s, me_k],
                device_id=device(s, k),
                device_id_type=MESH,
            ),
            lambda: pltpu.make_async_copy(src, dst, recv2.at[half, me_s, me_k]),
        )

    for b in range(blocks):
        bias = jnp.concatenate(
            [bias_ref[GRID - 1 + per_block * b - k] for k in range(GRID)], axis=0
        )
        for w in range(part):
            qbd = (
                jnp.concatenate(
                    [q_s[b, w, i] for i in range(per_block) for _ in range(head_count // 2)], axis=0
                )
                * mask_bf
            )
            s = lax.dot_general(
                k_s[w], qbd, (((1,), (1,)), ((), ())), preferred_element_type=jnp.float32
            )
            s = s + bias
            e = jnp.exp(s - jnp.max(s, axis=0, keepdims=True))
            p = (e * (1.0 / jnp.sum(e, axis=0, keepdims=True))).astype(jnp.bfloat16)
            o = lax.dot_general(
                p, v_s[w], (((0,), (0,)), ((), ())), preferred_element_type=jnp.float32
            )
            o = (o * mask).reshape(per_block, head_count, GRID, chans)
            ctx_s[w] = jnp.sum(o, axis=1).reshape(piece, chans).astype(jnp.bfloat16)
        ctx = dot(swap, ctx_s[...].reshape(span, chans)).astype(jnp.bfloat16)
        x = arr[per_block * b : per_block * (b + 1)].reshape(span, chans).astype(jnp.float32)
        attended = (x + dot(ctx, wout_ref[...])).astype(jnp.bfloat16)
        outb[per_block * b : per_block * (b + 1)] = attended.reshape(per_block, GRID, part, chans)
        for m in range(GRID):
            k = (me_k + m) % GRID
            s, remote, own = back_copy(b, k)

            @pl.when(jnp.logical_not(is_me(s, k)))
            def _():
                remote().start()

            @pl.when(is_me(s, k))
            def _():
                own().start()

    pairs = GRID // 2
    for m in range(pairs):
        pair = (me_k // 2 + m) % pairs
        for s in range(strips):
            for kk in range(2):
                k = 2 * pair + kk
                for half in range(blocks_per_strip):
                    ref = sec2.at[pl.ds(per_block * half, per_block), k, pl.ds(part * s, part)]
                    pltpu.make_async_copy(ref, ref, recv2.at[half, s, k]).wait()
        x = sec2[:, pl.ds(2 * pair, 2)].reshape(grid_rows * 2 * cols, chans).astype(jnp.float32)
        normed = layer_norm(x, fg_ref[...], fs_ref[...]).astype(jnp.bfloat16)
        hidden = gelu_tanh(dot(normed, wup_ref[...]) + bup_ref[...]).astype(jnp.bfloat16)
        res = x + dot(hidden, wdown_ref[...]) + bdown_ref[...]
        out_ref[:, pl.ds(2 * pair, 2)] = res.reshape(grid_rows, 2, cols, chans)

    for copy in halo:
        copy.wait_send()
    for s in range(strips):
        for k in range(GRID):

            @pl.when(jnp.logical_not(is_me(s, k)))
            def _():
                src = sec_ref.at[:, k, pl.ds(part * s, part)]
                dst = arr.at[pl.ds(grid_rows * me_s, grid_rows), me_k]
                pltpu.make_async_remote_copy(
                    src,
                    dst,
                    send1.at[s, k],
                    recv1.at[me_s, me_k],
                    device_id=device(s, k),
                    device_id_type=MESH,
                ).wait_send()

    for b in range(blocks):
        for k in range(GRID):
            s, remote, own = back_copy(b, k)

            @pl.when(jnp.logical_not(is_me(s, k)))
            def _():
                remote().wait_send()


def local(
    image,
    bn_gain,
    bn_shift,
    w_expand,
    b_expand,
    w_depth,
    b_depth,
    w_project,
    b_project,
    attn_gain,
    attn_shift,
    w_qkv,
    w_out,
    rel_table,
    ffn_gain,
    ffn_shift,
    w_up,
    b_up,
    w_down,
    b_down,
):
    tile_rows, tile_cols, channels = image.shape
    strips = lax.axis_size("strip")
    tile_count = lax.axis_size("tile")
    grid_rows = GRID // strips
    across = tile_rows // grid_rows
    col_groups = tile_count // GRID
    heads = rel_table.shape[0]
    part = tile_cols // strips
    piece = part
    blocks = GRID * GRID // piece
    bias = place_bias(rel_table)
    hidden = w_expand.shape[1]
    bf, f32 = jnp.bfloat16, jnp.float32
    vmem = pl.BlockSpec(memory_space=pltpu.VMEM)
    out = pl.pallas_call(
        functools.partial(block_kernel, strips, col_groups, heads),
        out_shape=jax.ShapeDtypeStruct((grid_rows, across, tile_cols, channels), f32),
        in_specs=[vmem] * 20,
        out_specs=vmem,
        scratch_shapes=[
            pltpu.VMEM((2, tile_rows, channels), bf),
            pltpu.VMEM((2, strips, tile_rows, channels), bf),
            pltpu.VMEM((2, tile_cols, channels), bf),
            pltpu.VMEM((2, strips * tile_rows + 16, hidden), f32),
            pltpu.VMEM((tile_rows + 2, hidden // 128, tile_cols + 16, 128), f32),
            pltpu.VMEM((4 * tile_cols, hidden), bf),
            pltpu.VMEM((grid_rows, across, tile_cols, channels), bf),
            pltpu.VMEM((GRID, GRID, part, channels), bf),
            pltpu.VMEM((blocks, part, piece // GRID, 2 * GRID, channels), bf),
            pltpu.VMEM((part, GRID * GRID, channels), bf),
            pltpu.VMEM((part, GRID * GRID, channels), bf),
            pltpu.VMEM((part, piece, channels), bf),
            pltpu.VMEM((GRID, GRID, part, channels), bf),
            pltpu.VMEM((grid_rows, GRID, tile_cols, channels), bf),
            pltpu.SemaphoreType.DMA((strips, GRID)),
            pltpu.SemaphoreType.DMA((strips, GRID)),
            pltpu.SemaphoreType.DMA((blocks, GRID)),
            pltpu.SemaphoreType.DMA((blocks // strips, strips, GRID)),
            pltpu.SemaphoreType.DMA((3, 2)),
            pltpu.SemaphoreType.DMA((3, 2)),
        ],
        compiler_params=pltpu.CompilerParams(collective_id=0, has_side_effects=True),
    )(
        image,
        bn_gain.reshape(1, -1),
        bn_shift.reshape(1, -1),
        w_expand,
        b_expand.reshape(1, -1),
        w_depth,
        b_depth.reshape(1, -1),
        w_project,
        b_project.reshape(1, -1),
        attn_gain.reshape(1, -1),
        attn_shift.reshape(1, -1),
        w_qkv,
        w_out,
        bias,
        ffn_gain.reshape(1, -1),
        ffn_shift.reshape(1, -1),
        w_up,
        b_up.reshape(1, -1),
        w_down,
        b_down.reshape(1, -1),
    )
    return out.astype(bf).reshape(tile_rows, tile_cols, channels)


def solution(mesh):
    return jax.shard_map(
        local,
        mesh=mesh,
        in_specs=(P(("group", "strip"), "tile", None),) + (P(),) * 19,
        out_specs=P(("group", "strip"), "tile", None),
        check_vma=False,
    )
```

profile of v0, /device:TPU:1, one launch (start us, length us, event | category | flops | bytes accessed | tf_op | source)
XLA Modules:
  0.0 49.4 jit_solution(9518084926340572344)
XLA Ops:
  0.0 0.0 copy-start
  0.0 0.7 %copy-done = f32[8,225]{1,0:T(8,128)S(1)} copy-done((f32[8,225]{1,0:T(8,128)S(1)}, f32[8,225]{1,0:T(8,128)}, u32[]{:S(2)}) %copy-start) | copy-done | bytes 7224
  0.7 0.1 reshape.56
  0.8 0.4 convolution_bitcast_fusion
  1.2 0.1 slice_bitcast_fusion.1
  1.4 0.1 copy.23
  1.5 0.1 copy.24
  1.6 0.7 %pad_maximum_fusion.bias_ref = f32[14,8,128]{2,1,0:T(8,128)} fusion(f32[14,8,64]{2,1,0:T(8,128)S(1)} %copy.24, f32[14,8,64]{2,1,0:T(8,128)S(1)} %copy.23), kind=kLoop, calls=%fused_computation.3 | loop fusion | flops 14336 | bytes 114688 | tf_op jit(solution)/shard_map/concatenate | solution.py:36
  2.4 44.9 %shard_map.190 = f32[4,8,32,256]{3,2,1,0:T(8,128)} custom-call(bf16[32,32,256]{2,1,0:T(8,128)(2,1)} %image_ref.1, f32[1,256]{1,0:T(1,128)} %bitcast.27, f32[1,256]{1,0:T(1,128)} %bitcast.28, bf16[256,1024]{1,0:T(8,128)(2,1)} %wexp_ref.1, f32[1,1024]{1,0:T(1,128)} %bitcast.24, f32[9,1024]{1,0:T(8,128)} %wdep_ref.1, f32[1,1024]{1,0:T(1,128)} %bitcast.25, ...), custom_call_target="tpu_custom_call" | custom-call | tf_op jit(solution)/shard_map/pallas_call | solution.py:422
  47.3 2.1 %convert_element_type.4 = bf16[4,8,32,256]{3,2,1,0:T(8,128)(2,1)} convert(f32[4,8,32,256]{3,2,1,0:T(8,128)} %shard_map.190) | non-fusion elementwise | flops 262144 | bytes 1572864 | tf_op jit(solution)/shard_map/convert_element_type | solution.py:472
  (1 shorter events, 0.0 us)
Async XLA Ops:
  0.0 0.7 %copy-start = (f32[8,225]{1,0:T(8,128)S(1)}, f32[8,225]{1,0:T(8,128)}, u32[]{:S(2)}) copy-start(f32[8,225]{1,0:T(8,128)} %param.33) | copy-start | bytes 21604
where the time goes:
time: 49.6 us; the launch traced here: 49.4 us
  Pallas kernels  44.9 us (91%)
  other arithmetic  2.82 us (6%)
  local copies, waits for them, and re-layouts  1.18 us (2%)
    pallas_call x1, Pallas kernels, local(): pl.pallas_call(functools.partial(block_kernel, strips, col_groups, heads)...  44.9 us
    convert_element_type x1, other arithmetic, local(): return out.astype(bf).reshape(tile_rows, tile_cols, channels)  2.1 us

commit v1 on v0

v1 whole, which is shorter than its diff:
```python
import functools
import math

import jax
import jax.numpy as jnp
from jax import lax
from jax.experimental import pallas as pl
from jax.experimental.pallas import tpu as pltpu
from jax.sharding import PartitionSpec as P

GRID = 8
EPSILON = 1e-05
LANES = 128
PACK = 16
PAD = 8
FAR = -1e6
MESH = pl.DeviceIdType.MESH

ROOT = math.sqrt(2.0 / math.pi)
SCALE = (ROOT * 0.044715) ** (1.0 / 3.0)
INNER = ROOT / SCALE
UNSCALE = 0.5 / SCALE
LOG2E = math.log2(math.e)


def scaled_gelu(z):
    return z + z * jnp.tanh(z * (z * z + INNER))


def layer_norm(inputs, norm_gain, norm_shift):
    center = jnp.mean(inputs, axis=-1, keepdims=True)
    spread = jnp.mean(jnp.square(inputs - center), axis=-1, keepdims=True)
    return (inputs - center) * lax.rsqrt(spread + EPSILON) * norm_gain + norm_shift


def dot(a, b):
    return jnp.dot(a, b, preferred_element_type=jnp.float32)


def dot_on(a, b, dims):
    return lax.dot_general(a, b, ((dims[:1], dims[1:]), ((), ())), preferred_element_type=jnp.float32)


def block_kernel(
    strips,
    col_groups,
    head_count,
    image_ref,
    bng_ref,
    bns_ref,
    wexp_ref,
    bexp_ref,
    wdep_ref,
    bdep_ref,
    wproj_hbm,
    bproj_ref,
    ag_ref,
    as_ref,
    wqkv_hbm,
    wout_hbm,
    table_ref,
    fg_ref,
    fs_ref,
    wup_hbm,
    bup_ref,
    wdown_hbm,
    bdown_ref,
    out_hbm,
    wproj_ref,
    wqkv_ref,
    wout_ref,
    wup_ref,
    wdown_ref,
    edge,
    cols_in,
    rows_in,
    xs,
    e_s,
    be_s,
    wd_s,
    h_s,
    sec,
    arr,
    tab_s,
    bias_s,
    swap_s,
    back_s,
    outb,
    sec2,
    ob,
    outv,
    wsem,
    send1,
    recv1,
    send2,
    recv2,
    hsend,
    hrecv,
    osem,
):
    bf, f32 = jnp.bfloat16, jnp.float32
    rows, cols, chans = image_ref.shape
    hidden = wexp_ref.shape[1]
    groups = cols // GRID
    width = cols + 2 * PAD
    peers = strips * GRID
    kinds = strips + 2
    span = peers * PACK
    mine = GRID // strips
    places = GRID * GRID
    head_size = chans // head_count
    halves = chans // LANES
    half_heads = LANES // head_size
    me_s = lax.axis_index("strip")
    tile = lax.axis_index("tile")
    me_k = tile // col_groups
    within = tile % col_groups
    me_u = me_s * GRID + me_k

    def device(s, k):
        return {"strip": s, "tile": k * col_groups + within}

    barrier = pltpu.get_barrier_semaphore()
    for m in range(1, peers):
        s, k = (me_s + m // GRID) % strips, (me_k + m) % GRID
        pl.semaphore_signal(barrier, inc=1, device_id=device(s, k), device_id_type=MESH)
    tiles = GRID * col_groups
    sides = ((tile + tiles - 1) % tiles, (tile + 1) % tiles)
    for t in sides:
        for s in range(strips):
            pl.semaphore_signal(
                barrier, inc=1, device_id={"strip": s, "tile": t}, device_id_type=MESH
            )

    weights = [
        pltpu.make_async_copy(src, dst, wsem.at[i])
        for i, (src, dst) in enumerate(
            (
                (wproj_hbm, wproj_ref),
                (wqkv_hbm, wqkv_ref),
                (wout_hbm, wout_ref),
                (wup_hbm, wup_ref),
                (wdown_hbm, wdown_ref),
            )
        )
    ]
    for copy in weights:
        copy.start()

    def put(at, value):
        for f in range(halves):
            xs[f, at, :] = value[:, LANES * f : LANES * (f + 1)]

    def take(at, count, stride):
        return jnp.concatenate(
            [xs[f, pl.ds(at, count, stride=stride), :] for f in range(halves)], axis=1
        )

    @pl.loop(0, rows)
    def _(r):
        at = pl.multiple_of((r + 1) * width + PAD, PAD)
        put(pl.ds(at, cols), image_ref[r].astype(f32))

    edge[0] = take(width + PAD, rows, width).astype(bf)
    edge[1] = take(width + PAD + cols - 1, rows, width).astype(bf)

    pl.semaphore_wait(barrier, peers - 1 + 2 * strips)

    halo = []
    for i in range(2):
        halo.append(
            pltpu.make_async_remote_copy(
                image_ref.at[(rows - 1) * (1 - i)],
                rows_in.at[i],
                hsend.at[2, i],
                hrecv.at[2, i],
                device_id={"strip": (me_s + 1 + i * (strips - 2)) % strips, "tile": tile},
                device_id_type=MESH,
            )
        )
    for i in range(2):
        for s in range(strips):
            halo.append(
                pltpu.make_async_remote_copy(
                    edge.at[i],
                    cols_in.at[1 - i, me_s],
                    hsend.at[i, s],
                    hrecv.at[1 - i, me_s],
                    device_id={"strip": s, "tile": sides[i]},
                    device_id_type=MESH,
                )
            )
    for copy in halo:
        copy.start()

    row16 = lax.broadcasted_iota(jnp.int32, (PACK, 1), 0)
    bexp = jnp.broadcast_to(bexp_ref[...] * SCALE, (PACK, hidden))
    for kk in range(kinds):
        be = bexp
        if kk == 0:
            be = be + jnp.where(row16 == 0, jnp.where(me_s == 0, FAR, 0.0), 0.0)
        if kk == kinds - 1:
            be = be + jnp.where(
                row16 == PACK - 1, jnp.where(me_s == strips - 1, FAR, 0.0), 0.0
            )
        be_s[kk] = be.astype(bf)
    for tap in range(9):
        wd_s[tap] = jnp.broadcast_to(wdep_ref[tap : tap + 1, :] * 0.5, (PACK, hidden)).astype(bf)
    wd_s[9] = jnp.broadcast_to(bdep_ref[...] * SCALE, (PACK, hidden)).astype(bf)

    for i in range(2):
        pltpu.make_async_copy(rows_in.at[i], rows_in.at[i], hrecv.at[2, i]).wait()
        at = PAD + (rows + 1) * width * i
        put(pl.ds(at, cols), rows_in[i].astype(f32))

    bng = bng_ref[...] * SCALE
    bns = bns_ref[...] * SCALE
    step = strips * width

    def expand(first, count):
        @pl.loop(0, count)
        def _(q):
            at = first + 2 * q
            lhs = []
            for cc in range(2):
                for kk in range(kinds):
                    raw = take(kk * width + PAD - 1 + at + cc, PACK, step)
                    lhs.append((raw * bng + bns).astype(bf))
            lhs = jnp.concatenate(lhs, axis=0)
            for n in range(hidden // 256):
                lanes = slice(256 * n, 256 * (n + 1))
                z = dot(lhs, wexp_ref[:, lanes]).astype(bf)
                for cc in range(2):
                    for kk in range(kinds):
                        i = cc * kinds + kk
                        zi = z[PACK * i : PACK * (i + 1)] + be_s[kk, :, lanes]
                        e_s[at + cc, kk, :, lanes] = scaled_gelu(zi)

    expand(GRID, 1)

    def first_send(j):
        sends = []
        for m in order:
            s, k = (me_s + m // GRID) % strips, (me_k + m) % GRID
            sends.append(
                pltpu.make_async_remote_copy(
                    sec.at[j, s * GRID + k],
                    arr.at[j, me_u],
                    send1.at[j],
                    recv1.at[j],
                    device_id=device(s, k),
                    device_id_type=MESH,
                )
            )
        return sends, pltpu.make_async_copy(sec.at[j, me_u], arr.at[j, me_u], recv1.at[j])

    def back_send(j):
        sends = []
        for m in order:
            s, k = (me_s + m // GRID) % strips, (me_k + m) % GRID
            sends.append(
                pltpu.make_async_remote_copy(
                    outb.at[j, s * GRID + k],
                    sec2.at[j, me_u],
                    send2.at[j],
                    recv2.at[j],
                    device_id=device(s, k),
                    device_id_type=MESH,
                )
            )
        return sends, pltpu.make_async_copy(outb.at[j, me_u], sec2.at[j, me_u], recv2.at[j])

    half = GRID // 2
    order = [m for m in range(1, peers)]
    order.sort(key=lambda m: abs(m % GRID - half))

    def flag(ok):
        return jnp.broadcast_to(jnp.where(ok, 1.0, 0.0), (PACK, hidden)).astype(bf)

    for j in range(groups):
        start = (GRID * (j + 1) + 2) % (cols + 2)
        if j == groups - 2:
            for i in range(2):
                for s in range(strips):
                    pltpu.make_async_copy(cols_in.at[i, s], cols_in.at[i, s], hrecv.at[i, s]).wait()
            for i in range(2):
                at = PAD - 1 + (cols + 1) * i
                put(pl.ds(width + at, rows, stride=width), cols_in[i, me_s].astype(f32))
                above = cols_in[i, (me_s + strips - 1) % strips].astype(f32)
                put(pl.ds(at, 1), above[rows - 1 : rows])
                below = cols_in[i, (me_s + 1) % strips].astype(f32)
                low = (rows + 1) * width + at
                put(pl.ds(low, 1), below[0:1])
        expand(start, GRID // 2)
        if j == groups - 2:
            ok = flag(tile < tiles - 1)
            for kk in range(kinds):
                e_s[cols + 1, kk] = e_s[cols + 1, kk] * ok
        if j == groups - 1:
            ok = flag(tile > 0)
            for kk in range(kinds):
                e_s[0, kk] = e_s[0, kk] * ok
        base = GRID * ((j + 1) % groups)

        @pl.loop(0, GRID // 2)
        def _(q):
            for c in range(hidden // LANES):
                lanes = slice(LANES * c, LANES * (c + 1))
                taps = [wd_s[t, :, lanes] for t in range(10)]
                for cc in range(2):
                    at = base + 2 * q + cc
                    for kk in range(strips):
                        acc = taps[9]
                        for a in range(3):
                            for b in range(3):
                                acc = acc + e_s[at + b, kk + a, :, lanes] * taps[3 * a + b]
                        h_s[kk, 2 * q + cc, :, lanes] = scaled_gelu(acc)

        if j == 0:
            weights[0].wait()
        skip = jnp.concatenate(
            [
                take((kk + 1) * width + PAD + base + c, PACK, step)
                for kk in range(strips)
                for c in range(GRID)
            ],
            axis=0,
        )
        proj = dot(h_s[...].reshape(span, hidden), wproj_ref[...])
        out = skip + proj * UNSCALE + bproj_ref[...]
        sec[j] = out.astype(bf).reshape(peers, PACK, chans)
        sends, own = first_send(j)
        for copy in sends:
            copy.start()
        own.start()

    side = 2 * GRID - 1
    slot = 2 * GRID
    tab_s[...] = jnp.zeros_like(tab_s)
    tab_s[:, 0 : side * side] = table_ref[...] * LOG2E
    table = tab_s[...]
    lane = lax.broadcasted_iota(jnp.int32, (head_count, LANES), 1)
    sub = lax.broadcasted_iota(jnp.int32, (head_count, LANES), 0)
    in_pair = LANES // (half_heads * slot)
    for f in range(halves):
        keep = sub == half_heads * f + lane // slot % half_heads
        even, odd = [], []
        for d in range(side):
            x = pltpu.roll(table, (table.shape[1] - side * d) % table.shape[1], 1)[:, :LANES]
            x = jnp.where(lane < side, x, 0.0)
            n = slot
            while n < LANES:
                x = x + pltpu.roll(x, n, 1)
                n *= 2
            x = jnp.sum(jnp.where(keep, x, 0.0), axis=0, keepdims=True)
            x = jnp.broadcast_to(x, (GRID, LANES))
            x = pltpu.roll(x, LANES - (GRID - 1), 1, stride=1, stride_axis=0)
            even.append(x)
            odd.append(pltpu.roll(x, GRID, 1))
        lane8 = lax.broadcasted_iota(jnp.int32, (GRID, LANES), 1)
        first = lane8 % slot < GRID
        pair_of = lane8 // (half_heads * slot)
        tiles_by = []
        for d in range(side - 2 * in_pair + 1):
            tile_bias = jnp.where(first, even[d], odd[d + 1])
            for b in range(1, in_pair):
                more = jnp.where(first, even[d + 2 * b], odd[d + 2 * b + 1])
                tile_bias = jnp.where(pair_of == b, more, tile_bias)
            tiles_by.append(tile_bias)
        for g in range(GRID // 2 // in_pair):
            for r in range(GRID):
                bias_s[f, GRID * r : GRID * (r + 1), LANES * g : LANES * (g + 1)] = tiles_by[
                    GRID - 1 + 2 * in_pair * g - r
                ]

    row_id = lax.broadcasted_iota(jnp.int32, (span, span), 0)
    col_id = lax.broadcasted_iota(jnp.int32, (span, span), 1)

    def place_of(n):
        p = n % PACK
        s, k = n // PACK // GRID, n // PACK % GRID
        grid_row = (rows // GRID) * s + p // mine
        return p % mine * places + grid_row * GRID + k

    swap_s[...] = jnp.where(row_id == place_of(col_id), 1.0, 0.0).astype(bf)
    back_s[...] = jnp.where(col_id == place_of(row_id), 1.0, 0.0).astype(bf)
    lane16 = lax.broadcasted_iota(jnp.int32, (PACK, LANES), 1) // head_size
    masks = [jnp.where(lane16 == h, 1.0, 0.0).astype(bf) for h in range(half_heads)]
    weights[1].wait()
    weights[2].wait()
    pairs = places // PACK

    @pl.loop(0, groups)
    def _(j):
        pltpu.make_async_copy(arr.at[j], arr.at[j], recv1.at[j]).wait()
        x = arr[j].reshape(span, chans).astype(f32)
        normed = layer_norm(x, ag_ref[...], as_ref[...]).astype(bf)
        normed = dot(swap_s[...], normed).astype(bf)
        q = (dot(normed, wqkv_ref[:, 0:chans]) * (head_size**-0.5 * LOG2E)).astype(bf)
        key = dot(normed, wqkv_ref[:, chans : 2 * chans]).astype(bf)
        val = dot(normed, wqkv_ref[:, 2 * chans :]).astype(bf)
        ctx = []
        for w in range(mine):
            parts = []
            for f in range(halves):
                at = (slice(places * w, places * (w + 1)), slice(LANES * f, LANES * (f + 1)))
                qh, kh, vh = q[at], key[at], val[at]
                qbd = jnp.concatenate(
                    [
                        qh[PACK * b : PACK * (b + 1)] * masks[h]
                        for b in range(pairs)
                        for h in range(half_heads)
                    ],
                    axis=0,
                )
                s = dot_on(kh, qbd, (1, 1)) + bias_s[f]
                e = jnp.exp2(s - jnp.max(s, axis=0, keepdims=True))
                p = (e * (1.0 / jnp.sum(e, axis=0, keepdims=True))).astype(bf)
                o = dot_on(p, vh, (0, 0)).reshape(pairs, half_heads, PACK, LANES)
                pick = o[:, 0]
                here = lax.broadcasted_iota(jnp.int32, pick.shape, 2) // head_size
                for h in range(1, half_heads):
                    pick = jnp.where(here == h, o[:, h], pick)
                parts.append(pick.reshape(places, LANES).astype(bf))
            ctx.append(jnp.concatenate(parts, axis=1))
        ctx = dot(back_s[...], jnp.concatenate(ctx, axis=0)).astype(bf)
        attended = (x + dot(ctx, wout_ref[...])).astype(bf)
        outb[j] = attended.reshape(peers, PACK, chans)
        sends, own = back_send(j)
        for copy in sends:
            copy.start()
        own.start()

    weights[3].wait()
    weights[4].wait()

    @pl.loop(0, groups)
    def _(j):
        pltpu.make_async_copy(sec2.at[j], sec2.at[j], recv2.at[j]).wait()
        x = sec2[j].reshape(span, chans).astype(f32)
        normed = layer_norm(x, fg_ref[...] * SCALE, fs_ref[...] * SCALE).astype(bf)
        bup = jnp.broadcast_to(bup_ref[...] * SCALE, (PACK, hidden)).astype(bf)
        for n in range(hidden // 256):
            lanes = slice(256 * n, 256 * (n + 1))
            z = dot(normed, wup_ref[:, lanes]).astype(bf).reshape(strips, GRID, PACK, 256)
            h_s[:, :, :, lanes] = scaled_gelu(z + bup[:, lanes])
        res = dot(h_s[...].reshape(span, hidden), wdown_ref[...]) * UNSCALE
        res = x + res + bdown_ref[...]
        for kk in range(strips):
            for c in range(GRID):
                i = kk * GRID + c
                for f in range(halves):
                    ob[f, pl.ds(i, PACK, stride=peers), :] = res[
                        PACK * i : PACK * (i + 1), LANES * f : LANES * (f + 1)
                    ]
        outv[j] = jnp.concatenate(
            [ob[f].astype(bf).reshape(rows, GRID, LANES) for f in range(halves)], axis=-1
        )
        at = pl.multiple_of(GRID * ((j + 1) % groups), GRID)
        pltpu.make_async_copy(outv.at[j], out_hbm.at[:, pl.ds(at, GRID), :], osem.at[j]).start()

    for copy in halo:
        copy.wait_send()
    for j in range(groups):
        for ref, sem in ((sec, send1), (outb, send2)):
            sent = ref.at[j, pl.ds(0, peers - 1)]
            pltpu.make_async_copy(sent, sent, sem.at[j]).wait()
        pltpu.make_async_copy(outv.at[j], outv.at[j], osem.at[j]).wait()


def local(
    image,
    bn_gain,
    bn_shift,
    w_expand,
    b_expand,
    w_depth,
    b_depth,
    w_project,
    b_project,
    attn_gain,
    attn_shift,
    w_qkv,
    w_out,
    rel_table,
    ffn_gain,
    ffn_shift,
    w_up,
    b_up,
    w_down,
    b_down,
):
    rows, cols, chans = image.shape
    strips = lax.axis_size("strip")
    col_groups = lax.axis_size("tile") // GRID
    heads = rel_table.shape[0]
    hidden = w_expand.shape[1]
    groups = cols // GRID
    peers = strips * GRID
    span = peers * PACK
    assert rows == strips * PACK and cols % GRID == 0 and hidden == w_up.shape[1]
    bf, f32 = jnp.bfloat16, jnp.float32
    vmem = pl.BlockSpec(memory_space=pltpu.VMEM)
    hbm = pl.BlockSpec(memory_space=pl.ANY)
    held = {7, 11, 12, 16, 18}
    unit = (groups, peers, PACK, chans)
    return pl.pallas_call(
        functools.partial(block_kernel, strips, col_groups, heads),
        out_shape=jax.ShapeDtypeStruct(image.shape, bf),
        in_specs=[hbm if i in held else vmem for i in range(20)],
        out_specs=hbm,
        scratch_shapes=[
            pltpu.VMEM(w_project.shape, bf),
            pltpu.VMEM(w_qkv.shape, bf),
            pltpu.VMEM(w_out.shape, bf),
            pltpu.VMEM(w_up.shape, bf),
            pltpu.VMEM(w_down.shape, bf),
            pltpu.VMEM((2, rows, chans), bf),
            pltpu.VMEM((2, strips, rows, chans), bf),
            pltpu.VMEM((2, cols, chans), bf),
            pltpu.VMEM((chans // LANES, (rows + 2) * (cols + 2 * PAD), LANES), f32),
            pltpu.VMEM((cols + 2, strips + 2, PACK, hidden), bf),
            pltpu.VMEM((strips + 2, PACK, hidden), bf),
            pltpu.VMEM((10, PACK, hidden), bf),
            pltpu.VMEM((strips, GRID, PACK, hidden), bf),
            pltpu.VMEM(unit, bf),
            pltpu.VMEM(unit, bf),
            pltpu.VMEM((heads, 256), f32),
            pltpu.VMEM((chans // LANES, GRID * GRID, 256), f32),
            pltpu.VMEM((span, span), bf),
            pltpu.VMEM((span, span), bf),
            pltpu.VMEM(unit, bf),
            pltpu.VMEM(unit, bf),
            pltpu.VMEM((chans // LANES, span, LANES), f32),
            pltpu.VMEM((groups, rows, GRID, chans), bf),
            pltpu.SemaphoreType.DMA((5,)),
            pltpu.SemaphoreType.DMA((groups,)),
            pltpu.SemaphoreType.DMA((groups,)),
            pltpu.SemaphoreType.DMA((groups,)),
            pltpu.SemaphoreType.DMA((groups,)),
            pltpu.SemaphoreType.DMA((3, 2)),
            pltpu.SemaphoreType.DMA((3, 2)),
            pltpu.SemaphoreType.DMA((groups,)),
        ],
        compiler_params=pltpu.CompilerParams(collective_id=0, has_side_effects=True),
    )(
        image,
        bn_gain.reshape(1, -1),
        bn_shift.reshape(1, -1),
        w_expand,
        b_expand.reshape(1, -1),
        w_depth,
        b_depth.reshape(1, -1),
        w_project,
        b_project.reshape(1, -1),
        attn_gain.reshape(1, -1),
        attn_shift.reshape(1, -1),
        w_qkv,
        w_out,
        rel_table,
        ffn_gain.reshape(1, -1),
        ffn_shift.reshape(1, -1),
        w_up,
        b_up.reshape(1, -1),
        w_down,
        b_down.reshape(1, -1),
    )


def solution(mesh):
    return jax.shard_map(
        local,
        mesh=mesh,
        in_specs=(P(("group", "strip"), "tile", None),) + (P(),) * 19,
        out_specs=P(("group", "strip"), "tile", None),
        check_vma=False,
    )
```

time: 49.6 us -> 38.8 us (0.78)
  Pallas kernels: 44.9 us -> 36.4 us
  other arithmetic: 2.82 us -> 0 us
  local copies, waits for them, and re-layouts: 1.18 us -> 1.87 us
    pallas_call x1, Pallas kernels: 44.9 us -> 36.4 us  [local(): pl.pallas_call(functools.partial(block_kernel, strips, col_groups, heads)...]
    convert_element_type x1 -> x0, other arithmetic: 2.1 us -> none  [local(): return out.astype(bf).reshape(tile_rows, tile_cols, channels)]
    unnamed x2 -> x1, local copies, waits for them, and re-layouts: 0.69 us -> 1.87 us
    concatenate x1 -> x0, other arithmetic: 0.72 us -> none  [place_bias(): return jnp.concatenate([by_col[:-1], by_col[1:]], axis=-1)]
where the time goes in v1:
time: 38.8 us; the launch traced here: 38.2 us
  Pallas kernels  36.4 us (94%)
  local copies, waits for them, and re-layouts  1.87 us (5%)
    pallas_call x1, Pallas kernels, local(): pl.pallas_call(functools.partial(block_kernel, strips, col_groups, heads)...  36.4 us
    unnamed x1, local copies, waits for them, and re-layouts  1.87 us

profile of v1, /device:TPU:1, one launch (start us, length us, event | category | flops | bytes accessed | tf_op | source)
XLA Modules:
  0.0 38.2 jit_solution(10544783276324753523)
XLA Ops:
  0.0 36.4 %shard_map.190 = bf16[32,32,256]{2,1,0:T(8,128)(2,1)} custom-call(bf16[32,32,256]{2,1,0:T(8,128)(2,1)} %image_ref.1, f32[1,256]{1,0:T(1,128)} %bitcast.14, f32[1,256]{1,0:T(1,128)} %bitcast.15, bf16[256,1024]{1,0:T(8,128)(2,1)} %wexp_ref.1, f32[1,1024]{1,0:T(1,128)} %bitcast.11, f32[9,1024]{1,0:T(8,128)} %wdep_ref.1, f32[1,1024]{1,0:T(1,128)} %bitcast.12, ...), custom_call_target="tpu_custom_call" | custom-call | tf_op jit(solution)/shard_map/pallas_call | solution.py:507
  36.4 1.9 %copy.22 = bf16[32,32,256]{2,1,0:T(8,128)(2,1)} copy(bf16[32,32,256]{2,1,0:T(8,128)(2,1)} %shard_map.190) | data formatting | bytes 1048576

commit v2 on v1

--- a/solution.py
+++ b/solution.py
@@ -3,6 +3,7 @@
 
 import jax
 import jax.numpy as jnp
+import numpy as np
 from jax import lax
 from jax.experimental import pallas as pl
 from jax.experimental.pallas import tpu as pltpu
@@ -12,8 +13,6 @@
 EPSILON = 1e-05
 LANES = 128
 PACK = 16
-PAD = 8
-FAR = -1e6
 MESH = pl.DeviceIdType.MESH
 
 ROOT = math.sqrt(2.0 / math.pi)
@@ -45,10 +44,10 @@
     strips,
     col_groups,
     head_count,
-    image_ref,
+    image_hbm,
     bng_ref,
     bns_ref,
-    wexp_ref,
+    wexp_hbm,
     bexp_ref,
     wdep_ref,
     bdep_ref,
@@ -65,29 +64,30 @@
     bup_ref,
     wdown_hbm,
     bdown_ref,
+    perm_hbm,
+    rim_ref,
+    corner_ref,
     out_hbm,
+    image_ref,
+    wexp_ref,
+    perm_ref,
     wproj_ref,
     wqkv_ref,
     wout_ref,
     wup_ref,
     wdown_ref,
-    edge,
     cols_in,
     rows_in,
-    xs,
+    u_s,
     e_s,
-    be_s,
     wd_s,
     h_s,
     sec,
     arr,
     tab_s,
     bias_s,
-    swap_s,
-    back_s,
     outb,
     sec2,
-    ob,
     outv,
     wsem,
     send1,
@@ -102,7 +102,6 @@
     rows, cols, chans = image_ref.shape
     hidden = wexp_ref.shape[1]
     groups = cols // GRID
-    width = cols + 2 * PAD
     peers = strips * GRID
     kinds = strips + 2
     span = peers * PACK
@@ -120,6 +119,24 @@
     def device(s, k):
         return {"strip": s, "tile": k * col_groups + within}
 
+    loads = [
+        pltpu.make_async_copy(src, dst, wsem.at[i])
+        for i, (src, dst) in enumerate(
+            (
+                (image_hbm, image_ref),
+                (perm_hbm, perm_ref),
+                (wexp_hbm, wexp_ref),
+                (wproj_hbm, wproj_ref),
+                (wqkv_hbm, wqkv_ref),
+                (wout_hbm, wout_ref),
+                (wup_hbm, wup_ref),
+                (wdown_hbm, wdown_ref),
+            )
+        )
+    ]
+    for copy in loads:
+        copy.start()
+
     barrier = pltpu.get_barrier_semaphore()
     for m in range(1, peers):
         s, k = (me_s + m // GRID) % strips, (me_k + m) % GRID
@@ -132,37 +149,16 @@
                 barrier, inc=1, device_id={"strip": s, "tile": t}, device_id_type=MESH
             )
 
-    weights = [
-        pltpu.make_async_copy(src, dst, wsem.at[i])
-        for i, (src, dst) in enumerate(
-            (
-                (wproj_hbm, wproj_ref),
-                (wqkv_hbm, wqkv_ref),
-                (wout_hbm, wout_ref),
-                (wup_hbm, wup_ref),
-                (wdown_hbm, wdown_ref),
-            )
+    def block(g):
+        return image_ref[:, GRID * g : GRID * (g + 1), :].reshape(rows * GRID, chans)
+
+    loads[0].wait()
+    loads[1].wait()
+    for g in range(groups):
+        units = dot(perm_ref[0], block(g)).astype(bf)
+        u_s[GRID * g + 1 : GRID * (g + 1) + 1, 1 : strips + 1] = units.reshape(
+            GRID, strips, PACK, chans
         )
-    ]
-    for copy in weights:
-        copy.start()
-
-    def put(at, value):
-        for f in range(halves):
-            xs[f, at, :] = value[:, LANES * f : LANES * (f + 1)]
-
-    def take(at, count, stride):
-        return jnp.concatenate(
-            [xs[f, pl.ds(at, count, stride=stride), :] for f in range(halves)], axis=1
-        )
-
-    @pl.loop(0, rows)
-    def _(r):
-        at = pl.multiple_of((r + 1) * width + PAD, PAD)
-        put(pl.ds(at, cols), image_ref[r].astype(f32))
-
-    edge[0] = take(width + PAD, rows, width).astype(bf)
-    edge[1] = take(width + PAD + cols - 1, rows, width).astype(bf)
 
     pl.semaphore_wait(barrier, peers - 1 + 2 * strips)
 
@@ -182,7 +178,7 @@
         for s in range(strips):
             halo.append(
                 pltpu.make_async_remote_copy(
-                    edge.at[i],
+                    u_s.at[1 + (cols - 1) * i, pl.ds(1, strips)],
                     cols_in.at[1 - i, me_s],
                     hsend.at[i, s],
                     hrecv.at[1 - i, me_s],
@@ -193,50 +189,47 @@
     for copy in halo:
         copy.start()
 
-    row16 = lax.broadcasted_iota(jnp.int32, (PACK, 1), 0)
-    bexp = jnp.broadcast_to(bexp_ref[...] * SCALE, (PACK, hidden))
-    for kk in range(kinds):
-        be = bexp
-        if kk == 0:
-            be = be + jnp.where(row16 == 0, jnp.where(me_s == 0, FAR, 0.0), 0.0)
-        if kk == kinds - 1:
-            be = be + jnp.where(
-                row16 == PACK - 1, jnp.where(me_s == strips - 1, FAR, 0.0), 0.0
-            )
-        be_s[kk] = be.astype(bf)
+    row16 = lax.broadcasted_iota(jnp.int32, (PACK, LANES * 2), 0)
+    bexp = jnp.broadcast_to(bexp_ref[...] * SCALE, (PACK, hidden)).astype(bf)
+    top = jnp.where(row16 == 0, jnp.where(me_s == 0, 0.0, 1.0), 1.0).astype(bf)
+    low = jnp.where(row16 == PACK - 1, jnp.where(me_s == strips - 1, 0.0, 1.0), 1.0).astype(bf)
     for tap in range(9):
-        wd_s[tap] = jnp.broadcast_to(wdep_ref[tap : tap + 1, :] * 0.5, (PACK, hidden)).astype(bf)
-    wd_s[9] = jnp.broadcast_to(bdep_ref[...] * SCALE, (PACK, hidden)).astype(bf)
+        wd_s[tap] = jnp.broadcast_to(wdep_ref[tap : tap + 1, :] * 0.5, (GRID, hidden)).astype(bf)
+    wd_s[9] = jnp.broadcast_to(bdep_ref[...] * SCALE, (GRID, hidden)).astype(bf)
 
     for i in range(2):
         pltpu.make_async_copy(rows_in.at[i], rows_in.at[i], hrecv.at[2, i]).wait()
-        at = PAD + (rows + 1) * width * i
-        put(pl.ds(at, cols), rows_in[i].astype(f32))
-
-    bng = bng_ref[...] * SCALE
-    bns = bns_ref[...] * SCALE
-    step = strips * width
-
-    def expand(first, count):
+    for g in range(groups):
+        beyond = rows_in[:, GRID * g : GRID * (g + 1), :].reshape(2 * GRID, chans)
+        units = (dot(perm_ref[1], block(g)) + dot(rim_ref[...], beyond)).astype(bf)
+        units = units.reshape(GRID, 2, PACK, chans)
+        at = slice(GRID * g + 1, GRID * (g + 1) + 1)
+        u_s[at, 0] = units[:, 0]
+        u_s[at, kinds - 1] = units[:, 1]
+
+    bng = jnp.broadcast_to(bng_ref[...] * SCALE, (PACK, chans)).astype(bf)
+    bns = jnp.broadcast_to(bns_ref[...] * SCALE, (PACK, chans)).astype(bf)
+    loads[2].wait()
+
+    def expand(first, batch, count):
         @pl.loop(0, count)
         def _(q):
-            at = first + 2 * q
-            lhs = []
-            for cc in range(2):
-                for kk in range(kinds):
-                    raw = take(kk * width + PAD - 1 + at + cc, PACK, step)
-                    lhs.append((raw * bng + bns).astype(bf))
-            lhs = jnp.concatenate(lhs, axis=0)
+            at = first + batch * q
+            raw = u_s[pl.ds(at, batch)].reshape(batch * kinds, PACK, chans)
+            lhs = (raw * bng + bns).reshape(batch * kinds * PACK, chans)
             for n in range(hidden // 256):
                 lanes = slice(256 * n, 256 * (n + 1))
-                z = dot(lhs, wexp_ref[:, lanes]).astype(bf)
-                for cc in range(2):
-                    for kk in range(kinds):
-                        i = cc * kinds + kk
-                        zi = z[PACK * i : PACK * (i + 1)] + be_s[kk, :, lanes]
-                        e_s[at + cc, kk, :, lanes] = scaled_gelu(zi)
-
-    expand(GRID, 1)
+                z = dot(lhs, wexp_ref[:, lanes]).astype(bf).reshape(batch, kinds, PACK, 256)
+                act = scaled_gelu(z + bexp[:, lanes])
+                for kk in range(kinds):
+                    a = act[:, kk]
+                    if kk == 0:
+                        a = a * top
+                    if kk == kinds - 1:
+                        a = a * low
+                    e_s[pl.ds(at, batch), kk, :, :, lanes] = a.reshape(batch, 2, GRID, 256)
+
+    expand(GRID, 2, 1)
 
     def first_send(j):
         sends = []
@@ -275,7 +268,7 @@
     order.sort(key=lambda m: abs(m % GRID - half))
 
     def flag(ok):
-        return jnp.broadcast_to(jnp.where(ok, 1.0, 0.0), (PACK, hidden)).astype(bf)
+        return jnp.broadcast_to(jnp.where(ok, 1.0, 0.0), (GRID, hidden)).astype(bf)
 
     for j in range(groups):
         start = (GRID * (j + 1) + 2) % (cols + 2)
@@ -284,14 +277,10 @@
                 for s in range(strips):
                     pltpu.make_async_copy(cols_in.at[i, s], cols_in.at[i, s], hrecv.at[i, s]).wait()
             for i in range(2):
-                at = PAD - 1 + (cols + 1) * i
-                put(pl.ds(width + at, rows, stride=width), cols_in[i, me_s].astype(f32))
-                above = cols_in[i, (me_s + strips - 1) % strips].astype(f32)
-                put(pl.ds(at, 1), above[rows - 1 : rows])
-                below = cols_in[i, (me_s + 1) % strips].astype(f32)
-                low = (rows + 1) * width + at
-                put(pl.ds(low, 1), below[0:1])
-        expand(start, GRID // 2)
+                rim = cols_in[i].reshape(strips * rows, chans)
+                units = dot(corner_ref[me_s], rim).astype(bf)
+                u_s[(cols + 1) * i] = units.reshape(kinds, PACK, chans)
+        expand(start, GRID // 2, 2)
         if j == groups - 2:
             ok = flag(tile < tiles - 1)
             for kk in range(kinds):
@@ -304,8 +293,8 @@
 
         @pl.loop(0, GRID // 2)
         def _(q):
-            for c in range(hidden // LANES):
-                lanes = slice(LANES * c, LANES * (c + 1))
+            for n in range(hidden // 256):
+                lanes = slice(256 * n, 256 * (n + 1))
                 taps = [wd_s[t, :, lanes] for t in range(10)]
                 for cc in range(2):
                     at = base + 2 * q + cc
@@ -313,19 +302,18 @@
                         acc = taps[9]
                         for a in range(3):
                             for b in range(3):
-                                acc = acc + e_s[at + b, kk + a, :, lanes] * taps[3 * a + b]
-                        h_s[kk, 2 * q + cc, :, lanes] = scaled_gelu(acc)
+                                acc = acc + e_s[at + b, kk + a, :, :, lanes] * taps[3 * a + b]
+                        h_s[kk, 2 * q + cc, :, :, lanes] = scaled_gelu(acc)
 
         if j == 0:
-            weights[0].wait()
+            loads[3].wait()
         skip = jnp.concatenate(
             [
-                take((kk + 1) * width + PAD + base + c, PACK, step)
+                u_s[base + 1 : base + GRID + 1, kk + 1].reshape(GRID * PACK, chans)
                 for kk in range(strips)
-                for c in range(GRID)
             ],
             axis=0,
-        )
+        ).astype(f32)
         proj = dot(h_s[...].reshape(span, hidden), wproj_ref[...])
         out = skip + proj * UNSCALE + bproj_ref[...]
         sec[j] = out.astype(bf).reshape(peers, PACK, chans)
@@ -373,21 +361,10 @@
                     GRID - 1 + 2 * in_pair * g - r
                 ]
 
-    row_id = lax.broadcasted_iota(jnp.int32, (span, span), 0)
-    col_id = lax.broadcasted_iota(jnp.int32, (span, span), 1)
-
-    def place_of(n):
-        p = n % PACK
-        s, k = n // PACK // GRID, n // PACK % GRID
-        grid_row = (rows // GRID) * s + p // mine
-        return p % mine * places + grid_row * GRID + k
-
-    swap_s[...] = jnp.where(row_id == place_of(col_id), 1.0, 0.0).astype(bf)
-    back_s[...] = jnp.where(col_id == place_of(row_id), 1.0, 0.0).astype(bf)
     lane16 = lax.broadcasted_iota(jnp.int32, (PACK, LANES), 1) // head_size
     masks = [jnp.where(lane16 == h, 1.0, 0.0).astype(bf) for h in range(half_heads)]
-    weights[1].wait()
-    weights[2].wait()
+    loads[4].wait()
+    loads[5].wait()
     pairs = places // PACK
 
     @pl.loop(0, groups)
@@ -395,7 +372,7 @@
         pltpu.make_async_copy(arr.at[j], arr.at[j], recv1.at[j]).wait()
         x = arr[j].reshape(span, chans).astype(f32)
         normed = layer_norm(x, ag_ref[...], as_ref[...]).astype(bf)
-        normed = dot(swap_s[...], normed).astype(bf)
+        normed = dot(perm_ref[2], normed).astype(bf)
         q = (dot(normed, wqkv_ref[:, 0:chans]) * (head_size**-0.5 * LOG2E)).astype(bf)
         key = dot(normed, wqkv_ref[:, chans : 2 * chans]).astype(bf)
         val = dot(normed, wqkv_ref[:, 2 * chans :]).astype(bf)
@@ -423,7 +400,7 @@
                     pick = jnp.where(here == h, o[:, h], pick)
                 parts.append(pick.reshape(places, LANES).astype(bf))
             ctx.append(jnp.concatenate(parts, axis=1))
-        ctx = dot(back_s[...], jnp.concatenate(ctx, axis=0)).astype(bf)
+        ctx = dot(perm_ref[3], jnp.concatenate(ctx, axis=0)).astype(bf)
         attended = (x + dot(ctx, wout_ref[...])).astype(bf)
         outb[j] = attended.reshape(peers, PACK, chans)
         sends, own = back_send(j)
@@ -431,8 +408,8 @@
             copy.start()
         own.start()
 
-    weights[3].wait()
-    weights[4].wait()
+    loads[6].wait()
+    loads[7].wait()
 
     @pl.loop(0, groups)
     def _(j):
@@ -442,20 +419,12 @@
         bup = jnp.broadcast_to(bup_ref[...] * SCALE, (PACK, hidden)).astype(bf)
         for n in range(hidden // 256):
             lanes = slice(256 * n, 256 * (n + 1))
-            z = dot(normed, wup_ref[:, lanes]).astype(bf).reshape(strips, GRID, PACK, 256)
-            h_s[:, :, :, lanes] = scaled_gelu(z + bup[:, lanes])
+            z = dot(normed, wup_ref[:, lanes]).astype(bf).reshape(peers, PACK, 256)
+            act = scaled_gelu(z + bup[:, lanes])
+            h_s[:, :, :, :, lanes] = act.reshape(strips, GRID, 2, GRID, 256)
         res = dot(h_s[...].reshape(span, hidden), wdown_ref[...]) * UNSCALE
         res = x + res + bdown_ref[...]
-        for kk in range(strips):
-            for c in range(GRID):
-                i = kk * GRID + c
-                for f in range(halves):
-                    ob[f, pl.ds(i, PACK, stride=peers), :] = res[
-                        PACK * i : PACK * (i + 1), LANES * f : LANES * (f + 1)
-                    ]
-        outv[j] = jnp.concatenate(
-            [ob[f].astype(bf).reshape(rows, GRID, LANES) for f in range(halves)], axis=-1
-        )
+        outv[j] = dot(perm_ref[4], res.astype(bf)).astype(bf).reshape(rows, GRID, chans)
         at = pl.multiple_of(GRID * ((j + 1) % groups), GRID)
         pltpu.make_async_copy(outv.at[j], out_hbm.at[:, pl.ds(at, GRID), :], osem.at[j]).start()
 
@@ -466,6 +435,43 @@
             sent = ref.at[j, pl.ds(0, peers - 1)]
             pltpu.make_async_copy(sent, sent, sem.at[j]).wait()
         pltpu.make_async_copy(outv.at[j], outv.at[j], osem.at[j]).wait()
+
+
+def permutations(strips, rows, grid_rows):
+    span = rows * GRID
+    mine = GRID // strips
+    out = np.zeros((5, span, span), np.float32)
+    rim = np.zeros((span, 2 * GRID), np.float32)
+    corner = np.zeros((strips, (strips + 2) * PACK, strips * rows), np.float32)
+    for c in range(GRID):
+        for p in range(PACK):
+            for k in range(strips):
+                row = (strips * p + k) * GRID + c
+                out[0, (c * strips + k) * PACK + p, row] = 1
+                out[4, row, (k * GRID + c) * PACK + p] = 1
+            if p > 0:
+                out[1, (2 * c) * PACK + p, (strips * p - 1) * GRID + c] = 1
+            else:
+                rim[(2 * c) * PACK + p, c] = 1
+            if p < PACK - 1:
+                out[1, (2 * c + 1) * PACK + p, strips * (p + 1) * GRID + c] = 1
+            else:
+                rim[(2 * c + 1) * PACK + p, GRID + c] = 1
+    for s in range(strips):
+        for k in range(strips + 2):
+            for p in range(PACK):
+                row = s * rows + strips * p + k - 1
+                if 0 <= row < strips * rows:
+                    far, within = row // rows, row % rows
+                    at = far * rows + within % strips * PACK + within // strips
+                    corner[s, k * PACK + p, at] = 1
+        for k in range(GRID):
+            for p in range(PACK):
+                token = (s * GRID + k) * PACK + p
+                place = p % mine * GRID * GRID + (grid_rows * s + p // mine) * GRID + k
+                out[2, place, token] = 1
+                out[3, token, place] = 1
+    return tuple(jnp.asarray(a, jnp.bfloat16) for a in (out, rim, corner))
 
 
 def local(
@@ -502,38 +508,37 @@
     bf, f32 = jnp.bfloat16, jnp.float32
     vmem = pl.BlockSpec(memory_space=pltpu.VMEM)
     hbm = pl.BlockSpec(memory_space=pl.ANY)
-    held = {7, 11, 12, 16, 18}
+    held = {0, 3, 7, 11, 12, 16, 18, 20}
+    perm, rim, corner = permutations(strips, rows, rows // GRID)
     unit = (groups, peers, PACK, chans)
     return pl.pallas_call(
         functools.partial(block_kernel, strips, col_groups, heads),
         out_shape=jax.ShapeDtypeStruct(image.shape, bf),
-        in_specs=[hbm if i in held else vmem for i in range(20)],
+        in_specs=[hbm if i in held else vmem for i in range(23)],
         out_specs=hbm,
         scratch_shapes=[
+            pltpu.VMEM(image.shape, bf),
+            pltpu.VMEM(w_expand.shape, bf),
+            pltpu.VMEM(perm.shape, bf),
             pltpu.VMEM(w_project.shape, bf),
             pltpu.VMEM(w_qkv.shape, bf),
             pltpu.VMEM(w_out.shape, bf),
             pltpu.VMEM(w_up.shape, bf),
             pltpu.VMEM(w_down.shape, bf),
-            pltpu.VMEM((2, rows, chans), bf),
-            pltpu.VMEM((2, strips, rows, chans), bf),
+            pltpu.VMEM((2, strips, strips, PACK, chans), bf),
             pltpu.VMEM((2, cols, chans), bf),
-            pltpu.VMEM((chans // LANES, (rows + 2) * (cols + 2 * PAD), LANES), f32),
-            pltpu.VMEM((cols + 2, strips + 2, PACK, hidden), bf),
-            pltpu.VMEM((strips + 2, PACK, hidden), bf),
-            pltpu.VMEM((10, PACK, hidden), bf),
-            pltpu.VMEM((strips, GRID, PACK, hidden), bf),
+            pltpu.VMEM((cols + 2, strips + 2, PACK, chans), bf),
+            pltpu.VMEM((cols + 2, strips + 2, 2, GRID, hidden), bf),
+            pltpu.VMEM((10, GRID, hidden), bf),
+            pltpu.VMEM((strips, GRID, 2, GRID, hidden), bf),
             pltpu.VMEM(unit, bf),
             pltpu.VMEM(unit, bf),
             pltpu.VMEM((heads, 256), f32),
             pltpu.VMEM((chans // LANES, GRID * GRID, 256), f32),
-            pltpu.VMEM((span, span), bf),
-            pltpu.VMEM((span, span), bf),
             pltpu.VMEM(unit, bf),
             pltpu.VMEM(unit, bf),
-            pltpu.VMEM((chans // LANES, span, LANES), f32),
             pltpu.VMEM((groups, rows, GRID, chans), bf),
-            pltpu.SemaphoreType.DMA((5,)),
+            pltpu.SemaphoreType.DMA((8,)),
             pltpu.SemaphoreType.DMA((groups,)),
             pltpu.SemaphoreType.DMA((groups,)),
             pltpu.SemaphoreType.DMA((groups,)),
@@ -564,6 +569,9 @@
         b_up.reshape(1, -1),
         w_down,
         b_down.reshape(1, -1),
+        perm,
+        rim,
+        corner,
     )
 
 

time: 38.8 us -> 37.8 us (0.974)
  Pallas kernels: 36.4 us -> 35.4 us
    pallas_call x1, Pallas kernels: 36.4 us -> 35.4 us  [local(): pl.pallas_call(functools.partial(block_kernel, strips, col_groups, heads)...]
where the time goes in v2:
time: 37.8 us; the launch traced here: 37.3 us
  Pallas kernels  35.4 us (94%)
  local copies, waits for them, and re-layouts  1.87 us (5%)
    pallas_call x1, Pallas kernels, local(): pl.pallas_call(functools.partial(block_kernel, strips, col_groups, heads)...  35.4 us
    unnamed x1, local copies, waits for them, and re-layouts  1.87 us

profile of v2, /device:TPU:1, one launch (start us, length us, event | category | flops | bytes accessed | tf_op | source)
XLA Modules:
  0.0 37.3 jit_solution(3861648367739781674)
XLA Ops:
  0.0 35.4 %shard_map.217 = bf16[32,32,256]{2,1,0:T(8,128)(2,1)} custom-call(bf16[32,32,256]{2,1,0:T(8,128)(2,1)} %image_hbm.1, f32[1,256]{1,0:T(1,128)} %bitcast.14, f32[1,256]{1,0:T(1,128)} %bitcast.15, bf16[256,1024]{1,0:T(8,128)(2,1)} %wexp_hbm.1, f32[1,1024]{1,0:T(1,128)} %bitcast.11, f32[9,1024]{1,0:T(8,128)} %wdep_ref.1, f32[1,1024]{1,0:T(1,128)} %bitcast.12, ...), custom_call_target="tpu_custom_call" | custom-call | tf_op jit(solution)/shard_map/pallas_call | solution.py:514
  35.4 1.9 %copy.25 = bf16[32,32,256]{2,1,0:T(8,128)(2,1)} copy(bf16[32,32,256]{2,1,0:T(8,128)(2,1)} %shard_map.217) | data formatting | bytes 1048576

commit v3 on v2

--- a/solution.py
+++ b/solution.py
@@ -13,6 +13,8 @@
 EPSILON = 1e-05
 LANES = 128
 PACK = 16
+OPERANDS = 23
+REACH = 2
 MESH = pl.DeviceIdType.MESH
 
 ROOT = math.sqrt(2.0 / math.pi)
@@ -44,60 +46,56 @@
     strips,
     col_groups,
     head_count,
-    image_hbm,
-    bng_ref,
-    bns_ref,
-    wexp_hbm,
-    bexp_ref,
-    wdep_ref,
-    bdep_ref,
-    wproj_hbm,
-    bproj_ref,
-    ag_ref,
-    as_ref,
-    wqkv_hbm,
-    wout_hbm,
-    table_ref,
-    fg_ref,
-    fs_ref,
-    wup_hbm,
-    bup_ref,
-    wdown_hbm,
-    bdown_ref,
-    perm_hbm,
-    rim_ref,
-    corner_ref,
-    out_hbm,
-    image_ref,
-    wexp_ref,
-    perm_ref,
-    wproj_ref,
-    wqkv_ref,
-    wout_ref,
-    wup_ref,
-    wdown_ref,
-    cols_in,
-    rows_in,
-    u_s,
-    e_s,
-    wd_s,
-    h_s,
-    sec,
-    arr,
-    tab_s,
-    bias_s,
-    outb,
-    sec2,
-    outv,
-    wsem,
-    send1,
-    recv1,
-    send2,
-    recv2,
-    hsend,
-    hrecv,
-    osem,
+    *refs,
 ):
+    operands, out_ref, held = refs[:OPERANDS], refs[OPERANDS], refs[OPERANDS + 1 : 2 * OPERANDS + 1]
+    (
+        image_ref,
+        bng_ref,
+        bns_ref,
+        wexp_ref,
+        bexp_ref,
+        wdep_ref,
+        bdep_ref,
+        wproj_ref,
+        bproj_ref,
+        ag_ref,
+        as_ref,
+        wqkv_ref,
+        wout_ref,
+        table_ref,
+        fg_ref,
+        fs_ref,
+        wup_ref,
+        bup_ref,
+        wdown_ref,
+        bdown_ref,
+        perm_ref,
+        rim_ref,
+        corner_ref,
+    ) = held
+    (
+        cols_in,
+        rows_in,
+        u_s,
+        e_s,
+        wd_s,
+        h_s,
+        sec,
+        arr,
+        tab_s,
+        bias_s,
+        outb,
+        sec2,
+        wsem,
+        send1,
+        recv1,
+        send2,
+        recv2,
+        hsend,
+        hrecv,
+        relay,
+    ) = refs[2 * OPERANDS + 1 :]
     bf, f32 = jnp.bfloat16, jnp.float32
     rows, cols, chans = image_ref.shape
     hidden = wexp_ref.shape[1]
@@ -119,48 +117,80 @@
     def device(s, k):
         return {"strip": s, "tile": k * col_groups + within}
 
+    half = GRID // 2
+    tiles = GRID * col_groups
     loads = [
         pltpu.make_async_copy(src, dst, wsem.at[i])
-        for i, (src, dst) in enumerate(
-            (
-                (image_hbm, image_ref),
-                (perm_hbm, perm_ref),
-                (wexp_hbm, wexp_ref),
-                (wproj_hbm, wproj_ref),
-                (wqkv_hbm, wqkv_ref),
-                (wout_hbm, wout_ref),
-                (wup_hbm, wup_ref),
-                (wdown_hbm, wdown_ref),
-            )
+        for i, (src, dst) in enumerate(zip(operands, held))
+    ]
+    early = (0, 20, 3, 1, 2, 4)
+    for i in early[:2]:
+        loads[i].start()
+
+    barrier = pltpu.get_barrier_semaphore()
+    for s in range(1, strips):
+        pl.semaphore_signal(
+            barrier, inc=1, device_id=device((me_s + s) % strips, me_k), device_id_type=MESH
         )
-    ]
-    for copy in loads:
-        copy.start()
-
-    barrier = pltpu.get_barrier_semaphore()
-    for m in range(1, peers):
-        s, k = (me_s + m // GRID) % strips, (me_k + m) % GRID
-        pl.semaphore_signal(barrier, inc=1, device_id=device(s, k), device_id_type=MESH)
-    tiles = GRID * col_groups
-    sides = ((tile + tiles - 1) % tiles, (tile + 1) % tiles)
-    for t in sides:
-        for s in range(strips):
-            pl.semaphore_signal(
-                barrier, inc=1, device_id={"strip": s, "tile": t}, device_id_type=MESH
-            )
+    expected = strips - 1
+    near = [d for r in range(REACH, 0, -1) for d in (r, -r)]
+    greet = [(me_k + d >= 0) & (me_k + d < GRID) for d in near]
+    greet = [(ok, (me_k + d) * col_groups + within) for d, ok in zip(near, greet)]
+    rim_sides = ((tile > 0, tile - 1), (tile < tiles - 1, tile + 1))
+    for ok, t in greet + list(rim_sides):
+        expected = expected + jnp.where(ok, strips, 0)
+
+        @pl.when(ok)
+        def _():
+            for s in range(strips):
+                pl.semaphore_signal(
+                    barrier, inc=1, device_id={"strip": s, "tile": t}, device_id_type=MESH
+                )
+
+    for i in early[2:]:
+        loads[i].start()
+    for i in range(OPERANDS):
+        if i not in early:
+            loads[i].start()
+
+    def spread(stage):
+        for i, d in enumerate((REACH, -REACH)):
+
+            @pl.when((me_k + d >= 0) & (me_k + d < GRID))
+            def _():
+                pl.semaphore_signal(
+                    relay.at[stage, i],
+                    inc=1,
+                    device_id=device(me_s, me_k + d),
+                    device_id_type=MESH,
+                )
+
+    def heard(stage):
+        for i, d in enumerate((-REACH, REACH)):
+
+            @pl.when((me_k + d >= 0) & (me_k + d < GRID))
+            def _():
+                pl.semaphore_wait(relay.at[stage, i], 1)
 
     def block(g):
         return image_ref[:, GRID * g : GRID * (g + 1), :].reshape(rows * GRID, chans)
 
     loads[0].wait()
-    loads[1].wait()
-    for g in range(groups):
-        units = dot(perm_ref[0], block(g)).astype(bf)
-        u_s[GRID * g + 1 : GRID * (g + 1) + 1, 1 : strips + 1] = units.reshape(
-            GRID, strips, PACK, chans
-        )
-
-    pl.semaphore_wait(barrier, peers - 1 + 2 * strips)
+    loads[20].wait()
+
+    def permute(g):
+        tokens = block(g)
+        at = slice(GRID * g + 1, GRID * (g + 1) + 1)
+        units = dot(perm_ref[0], tokens).astype(bf)
+        u_s[at, 0:strips] = units.reshape(GRID, strips, PACK, chans)
+        units = dot(perm_ref[1], tokens).astype(bf)
+        u_s[at, strips:kinds] = units.reshape(GRID, 2, PACK, chans)
+
+    for g in range(min(3, groups)):
+        permute(g)
+
+    pl.semaphore_wait(barrier, expected)
+    spread(0)
 
     halo = []
     for i in range(2):
@@ -174,67 +204,86 @@
                 device_id_type=MESH,
             )
         )
-    for i in range(2):
+    for copy in halo:
+        copy.start()
+    for g in range(3, groups):
+        permute(g)
+    rims = []
+    for i, (ok, t) in enumerate(rim_sides):
         for s in range(strips):
-            halo.append(
-                pltpu.make_async_remote_copy(
-                    u_s.at[1 + (cols - 1) * i, pl.ds(1, strips)],
-                    cols_in.at[1 - i, me_s],
-                    hsend.at[i, s],
-                    hrecv.at[1 - i, me_s],
-                    device_id={"strip": s, "tile": sides[i]},
-                    device_id_type=MESH,
+            rims.append(
+                (
+                    ok,
+                    pltpu.make_async_remote_copy(
+                        u_s.at[1 + (cols - 1) * i, pl.ds(0, strips)],
+                        cols_in.at[1 - i, me_s],
+                        hsend.at[i, s],
+                        hrecv.at[1 - i, me_s],
+                        device_id={"strip": s, "tile": t},
+                        device_id_type=MESH,
+                    ),
                 )
             )
-    for copy in halo:
-        copy.start()
-
+    for ok, copy in rims:
+
+        @pl.when(ok)
+        def _():
+            copy.start()
+
+    for i in early[2:]:
+        loads[i].wait()
     row16 = lax.broadcasted_iota(jnp.int32, (PACK, LANES * 2), 0)
     bexp = jnp.broadcast_to(bexp_ref[...] * SCALE, (PACK, hidden)).astype(bf)
     top = jnp.where(row16 == 0, jnp.where(me_s == 0, 0.0, 1.0), 1.0).astype(bf)
     low = jnp.where(row16 == PACK - 1, jnp.where(me_s == strips - 1, 0.0, 1.0), 1.0).astype(bf)
+    bng = jnp.broadcast_to(bng_ref[...] * SCALE, (PACK, chans)).astype(bf)
+    bns = jnp.broadcast_to(bns_ref[...] * SCALE, (PACK, chans)).astype(bf)
+
+    def expand(at, batch, kind, count):
+        raw = u_s[pl.ds(at, batch), kind : kind + count].reshape(batch * count, PACK, chans)
+        lhs = (raw * bng + bns).reshape(batch * count * PACK, chans)
+        for n in range(hidden // 256):
+            lanes = slice(256 * n, 256 * (n + 1))
+            z = dot(lhs, wexp_ref[:, lanes]).astype(bf).reshape(batch, count, PACK, 256)
+            act = scaled_gelu(z + bexp[:, lanes])
+            for c in range(count):
+                a = act[:, c]
+                if kind + c == strips:
+                    a = a * top
+                if kind + c == strips + 1:
+                    a = a * low
+                e_s[pl.ds(at, batch), kind + c, :, :, lanes] = a.reshape(batch, 2, GRID, 256)
+
+    far = (me_k // half + 1) % 2
+    batches = ((GRID + half * far, half + 2), (GRID + (half + 2) * (1 - far), half))
+    for at, batch in batches:
+        expand(at, batch, 0, strips)
+    for i in (5, 6):
+        loads[i].wait()
     for tap in range(9):
         wd_s[tap] = jnp.broadcast_to(wdep_ref[tap : tap + 1, :] * 0.5, (GRID, hidden)).astype(bf)
     wd_s[9] = jnp.broadcast_to(bdep_ref[...] * SCALE, (GRID, hidden)).astype(bf)
-
+    heard(0)
+    spread(1)
     for i in range(2):
         pltpu.make_async_copy(rows_in.at[i], rows_in.at[i], hrecv.at[2, i]).wait()
-    for g in range(groups):
+    loads[21].wait()
+
+    def add_rim(g):
         beyond = rows_in[:, GRID * g : GRID * (g + 1), :].reshape(2 * GRID, chans)
-        units = (dot(perm_ref[1], block(g)) + dot(rim_ref[...], beyond)).astype(bf)
-        units = units.reshape(GRID, 2, PACK, chans)
+        units = dot(rim_ref[...], beyond).astype(bf).reshape(GRID, 2, PACK, chans)
         at = slice(GRID * g + 1, GRID * (g + 1) + 1)
-        u_s[at, 0] = units[:, 0]
-        u_s[at, kinds - 1] = units[:, 1]
-
-    bng = jnp.broadcast_to(bng_ref[...] * SCALE, (PACK, chans)).astype(bf)
-    bns = jnp.broadcast_to(bns_ref[...] * SCALE, (PACK, chans)).astype(bf)
-    loads[2].wait()
-
-    def expand(first, batch, count):
-        @pl.loop(0, count)
-        def _(q):
-            at = first + batch * q
-            raw = u_s[pl.ds(at, batch)].reshape(batch * kinds, PACK, chans)
-            lhs = (raw * bng + bns).reshape(batch * kinds * PACK, chans)
-            for n in range(hidden // 256):
-                lanes = slice(256 * n, 256 * (n + 1))
-                z = dot(lhs, wexp_ref[:, lanes]).astype(bf).reshape(batch, kinds, PACK, 256)
-                act = scaled_gelu(z + bexp[:, lanes])
-                for kk in range(kinds):
-                    a = act[:, kk]
-                    if kk == 0:
-                        a = a * top
-                    if kk == kinds - 1:
-                        a = a * low
-                    e_s[pl.ds(at, batch), kk, :, :, lanes] = a.reshape(batch, 2, GRID, 256)
-
-    expand(GRID, 2, 1)
-
-    def first_send(j):
+        u_s[at, strips:kinds] = u_s[at, strips:kinds] + units
+
+    for g in range(min(3, groups)):
+        add_rim(g)
+    heard(1)
+    spread(2)
+
+    def first_send(j, h, own):
         sends = []
-        for m in order:
-            s, k = (me_s + m // GRID) % strips, (me_k + m) % GRID
+        for m in range(own, strips * half):
+            s, k = (me_s + m // half) % strips, half * h + (me_k + m) % half
             sends.append(
                 pltpu.make_async_remote_copy(
                     sec.at[j, s * GRID + k],
@@ -245,7 +294,10 @@
                     device_id_type=MESH,
                 )
             )
-        return sends, pltpu.make_async_copy(sec.at[j, me_u], arr.at[j, me_u], recv1.at[j])
+        return sends
+
+    def first_own(j):
+        return pltpu.make_async_copy(sec.at[j, me_u], arr.at[j, me_u], recv1.at[j])
 
     def back_send(j):
         sends = []
@@ -263,7 +315,6 @@
             )
         return sends, pltpu.make_async_copy(outb.at[j, me_u], sec2.at[j, me_u], recv2.at[j])
 
-    half = GRID // 2
     order = [m for m in range(1, peers)]
     order.sort(key=lambda m: abs(m % GRID - half))
 
@@ -272,15 +323,33 @@
 
     for j in range(groups):
         start = (GRID * (j + 1) + 2) % (cols + 2)
+        if j == 1:
+            for g in range(3, groups):
+                add_rim(g)
         if j == groups - 2:
-            for i in range(2):
-                for s in range(strips):
-                    pltpu.make_async_copy(cols_in.at[i, s], cols_in.at[i, s], hrecv.at[i, s]).wait()
+            loads[22].wait()
+            for i, (ok, _) in enumerate(rim_sides):
+
+                @pl.when(ok)
+                def _():
+                    for s in range(strips):
+                        ref = cols_in.at[i, s]
+                        pltpu.make_async_copy(ref, ref, hrecv.at[i, s]).wait()
+
+                @pl.when(jnp.logical_not(ok))
+                def _():
+                    cols_in[i] = jnp.zeros(cols_in.shape[1:], bf)
+
             for i in range(2):
                 rim = cols_in[i].reshape(strips * rows, chans)
                 units = dot(corner_ref[me_s], rim).astype(bf)
                 u_s[(cols + 1) * i] = units.reshape(kinds, PACK, chans)
-        expand(start, GRID // 2, 2)
+        if j > 0:
+
+            @pl.loop(0, 2)
+            def _(q):
+                expand(start + half * q, half, 0, kinds)
+
         if j == groups - 2:
             ok = flag(tile < tiles - 1)
             for kk in range(kinds):
@@ -291,40 +360,52 @@
                 e_s[0, kk] = e_s[0, kk] * ok
         base = GRID * ((j + 1) % groups)
 
-        @pl.loop(0, GRID // 2)
-        def _(q):
-            for n in range(hidden // 256):
-                lanes = slice(256 * n, 256 * (n + 1))
-                taps = [wd_s[t, :, lanes] for t in range(10)]
-                for cc in range(2):
-                    at = base + 2 * q + cc
-                    for kk in range(strips):
-                        acc = taps[9]
-                        for a in range(3):
-                            for b in range(3):
-                                acc = acc + e_s[at + b, kk + a, :, :, lanes] * taps[3 * a + b]
-                        h_s[kk, 2 * q + cc, :, :, lanes] = scaled_gelu(acc)
-
-        if j == 0:
-            loads[3].wait()
-        skip = jnp.concatenate(
-            [
-                u_s[base + 1 : base + GRID + 1, kk + 1].reshape(GRID * PACK, chans)
-                for kk in range(strips)
-            ],
-            axis=0,
-        ).astype(f32)
-        proj = dot(h_s[...].reshape(span, hidden), wproj_ref[...])
-        out = skip + proj * UNSCALE + bproj_ref[...]
-        sec[j] = out.astype(bf).reshape(peers, PACK, chans)
-        sends, own = first_send(j)
-        for copy in sends:
-            copy.start()
-        own.start()
+        for step in range(2):
+            h = (far + step) % 2
+            if j == 0:
+                expand(*batches[step], strips, 2)
+
+            @pl.loop(0, half // 2)
+            def _(q):
+                for n in range(hidden // 256):
+                    lanes = slice(256 * n, 256 * (n + 1))
+                    taps = [wd_s[t, :, lanes] for t in range(10)]
+                    for cc in range(2):
+                        at = base + half * h + 2 * q + cc
+                        for kk in range(strips):
+                            acc = taps[9]
+                            for a in range(3):
+                                kind = (kk + a - 1, strips, strips + 1)[
+                                    1 if kk + a == 0 else 2 if kk + a == strips + 1 else 0
+                                ]
+                                for b in range(3):
+                                    acc = acc + e_s[at + b, kind, :, :, lanes] * taps[3 * a + b]
+                            h_s[kk, 2 * q + cc, :, :, lanes] = scaled_gelu(acc)
+
+            if j == 0 and step == 0:
+                loads[7].wait()
+                loads[8].wait()
+            first = base + half * h + 1
+            skip = jnp.concatenate(
+                [u_s[pl.ds(first, half), kk].reshape(half * PACK, chans) for kk in range(strips)],
+                axis=0,
+            ).astype(f32)
+            act = h_s[:, 0:half].reshape(strips * half * PACK, hidden)
+            out = skip + dot(act, wproj_ref[...]) * UNSCALE + bproj_ref[...]
+            out = out.astype(bf).reshape(strips, half, PACK, chans)
+            for s in range(strips):
+                sec[j, pl.ds(s * GRID + half * h, half)] = out[s]
+            if j == 0 and step == 0:
+                heard(2)
+            for copy in first_send(j, h, step):
+                copy.start()
+            if step == 1:
+                first_own(j).start()
 
     side = 2 * GRID - 1
     slot = 2 * GRID
     tab_s[...] = jnp.zeros_like(tab_s)
+    loads[13].wait()
     tab_s[:, 0 : side * side] = table_ref[...] * LOG2E
     table = tab_s[...]
     lane = lax.broadcasted_iota(jnp.int32, (head_count, LANES), 1)
@@ -363,8 +444,8 @@
 
     lane16 = lax.broadcasted_iota(jnp.int32, (PACK, LANES), 1) // head_size
     masks = [jnp.where(lane16 == h, 1.0, 0.0).astype(bf) for h in range(half_heads)]
-    loads[4].wait()
-    loads[5].wait()
+    for i in (9, 10, 11, 12):
+        loads[i].wait()
     pairs = places // PACK
 
     @pl.loop(0, groups)
@@ -408,8 +489,8 @@
             copy.start()
         own.start()
 
-    loads[6].wait()
-    loads[7].wait()
+    for i in (14, 15, 16, 17, 18, 19):
+        loads[i].wait()
 
     @pl.loop(0, groups)
     def _(j):
@@ -424,17 +505,22 @@
             h_s[:, :, :, :, lanes] = act.reshape(strips, GRID, 2, GRID, 256)
         res = dot(h_s[...].reshape(span, hidden), wdown_ref[...]) * UNSCALE
         res = x + res + bdown_ref[...]
-        outv[j] = dot(perm_ref[4], res.astype(bf)).astype(bf).reshape(rows, GRID, chans)
+        final = dot(perm_ref[4], res.astype(bf)).astype(bf).reshape(rows, GRID, chans)
         at = pl.multiple_of(GRID * ((j + 1) % groups), GRID)
-        pltpu.make_async_copy(outv.at[j], out_hbm.at[:, pl.ds(at, GRID), :], osem.at[j]).start()
+        out_ref[:, pl.ds(at, GRID), :] = final
 
     for copy in halo:
         copy.wait_send()
+    for ok, copy in rims:
+
+        @pl.when(ok)
+        def _():
+            copy.wait_send()
+
     for j in range(groups):
         for ref, sem in ((sec, send1), (outb, send2)):
             sent = ref.at[j, pl.ds(0, peers - 1)]
             pltpu.make_async_copy(sent, sent, sem.at[j]).wait()
-        pltpu.make_async_copy(outv.at[j], outv.at[j], osem.at[j]).wait()
 
 
 def permutations(strips, rows, grid_rows):
@@ -459,8 +545,9 @@
                 rim[(2 * c + 1) * PACK + p, GRID + c] = 1
     for s in range(strips):
         for k in range(strips + 2):
+            shift = {strips: -1, strips + 1: strips}.get(k, k)
             for p in range(PACK):
-                row = s * rows + strips * p + k - 1
+                row = s * rows + strips * p + shift
                 if 0 <= row < strips * rows:
                     far, within = row // rows, row % rows
                     at = far * rows + within % strips * PACK + within // strips
@@ -508,47 +595,9 @@
     bf, f32 = jnp.bfloat16, jnp.float32
     vmem = pl.BlockSpec(memory_space=pltpu.VMEM)
     hbm = pl.BlockSpec(memory_space=pl.ANY)
-    held = {0, 3, 7, 11, 12, 16, 18, 20}
     perm, rim, corner = permutations(strips, rows, rows // GRID)
     unit = (groups, peers, PACK, chans)
-    return pl.pallas_call(
-        functools.partial(block_kernel, strips, col_groups, heads),
-        out_shape=jax.ShapeDtypeStruct(image.shape, bf),
-        in_specs=[hbm if i in held else vmem for i in range(23)],
-        out_specs=hbm,
-        scratch_shapes=[
-            pltpu.VMEM(image.shape, bf),
-            pltpu.VMEM(w_expand.shape, bf),
-            pltpu.VMEM(perm.shape, bf),
-            pltpu.VMEM(w_project.shape, bf),
-            pltpu.VMEM(w_qkv.shape, bf),
-            pltpu.VMEM(w_out.shape, bf),
-            pltpu.VMEM(w_up.shape, bf),
-            pltpu.VMEM(w_down.shape, bf),
-            pltpu.VMEM((2, strips, strips, PACK, chans), bf),
-            pltpu.VMEM((2, cols, chans), bf),
-            pltpu.VMEM((cols + 2, strips + 2, PACK, chans), bf),
-            pltpu.VMEM((cols + 2, strips + 2, 2, GRID, hidden), bf),
-            pltpu.VMEM((10, GRID, hidden), bf),
-            pltpu.VMEM((strips, GRID, 2, GRID, hidden), bf),
-            pltpu.VMEM(unit, bf),
-            pltpu.VMEM(unit, bf),
-            pltpu.VMEM((heads, 256), f32),
-            pltpu.VMEM((chans // LANES, GRID * GRID, 256), f32),
-            pltpu.VMEM(unit, bf),
-            pltpu.VMEM(unit, bf),
-            pltpu.VMEM((groups, rows, GRID, chans), bf),
-            pltpu.SemaphoreType.DMA((8,)),
-            pltpu.SemaphoreType.DMA((groups,)),
-            pltpu.SemaphoreType.DMA((groups,)),
-            pltpu.SemaphoreType.DMA((groups,)),
-            pltpu.SemaphoreType.DMA((groups,)),
-            pltpu.SemaphoreType.DMA((3, 2)),
-            pltpu.SemaphoreType.DMA((3, 2)),
-            pltpu.SemaphoreType.DMA((groups,)),
-        ],
-        compiler_params=pltpu.CompilerParams(collective_id=0, has_side_effects=True),
-    )(
+    operands = (
         image,
         bn_gain.reshape(1, -1),
         bn_shift.reshape(1, -1),
@@ -573,6 +622,37 @@
         rim,
         corner,
     )
+    call = pl.pallas_call(
+        functools.partial(block_kernel, strips, col_groups, heads),
+        out_shape=pltpu.VMEM(image.shape, bf),
+        in_specs=[hbm] * OPERANDS,
+        out_specs=vmem,
+        scratch_shapes=[
+            *(pltpu.VMEM(a.shape, a.dtype) for a in operands),
+            pltpu.VMEM((2, strips, strips, PACK, chans), bf),
+            pltpu.VMEM((2, cols, chans), bf),
+            pltpu.VMEM((cols + 2, strips + 2, PACK, chans), bf),
+            pltpu.VMEM((cols + 2, strips + 2, 2, GRID, hidden), bf),
+            pltpu.VMEM((10, GRID, hidden), bf),
+            pltpu.VMEM((strips, GRID, 2, GRID, hidden), bf),
+            pltpu.VMEM(unit, bf),
+            pltpu.VMEM(unit, bf),
+            pltpu.VMEM((heads, 256), f32),
+            pltpu.VMEM((chans // LANES, GRID * GRID, 256), f32),
+            pltpu.VMEM(unit, bf),
+            pltpu.VMEM(unit, bf),
+            pltpu.SemaphoreType.DMA((OPERANDS,)),
+            pltpu.SemaphoreType.DMA((groups,)),
+            pltpu.SemaphoreType.DMA((groups,)),
+            pltpu.SemaphoreType.DMA((groups,)),
+            pltpu.SemaphoreType.DMA((groups,)),
+            pltpu.SemaphoreType.DMA((3, 2)),
+            pltpu.SemaphoreType.DMA((3, 2)),
+            pltpu.SemaphoreType.REGULAR((-(-(GRID - 1) // REACH) - 1, 2)),
+        ],
+        compiler_params=pltpu.CompilerParams(collective_id=0, has_side_effects=True),
+    )
+    return call(*operands)
 
 
 def solution(mesh):

time: 37.8 us -> 34.7 us (0.918)
  Pallas kernels: 35.4 us -> 33.4 us
  local copies, waits for them, and re-layouts: 1.87 us -> 0.8 us
    pallas_call x1, Pallas kernels: 35.4 us -> 33.4 us  [local(): return call(*operands)]
    unnamed x1, local copies, waits for them, and re-layouts: 1.87 us -> 0.8 us
where the time goes in v3:
time: 34.7 us; the launch traced here: 34.2 us
  Pallas kernels  33.4 us (96%)
  local copies, waits for them, and re-layouts  0.8 us (2%)
    pallas_call x1, Pallas kernels, local(): return call(*operands)  33.4 us
    unnamed x1, local copies, waits for them, and re-layouts  0.8 us

profile of v3, /device:TPU:1, one launch (start us, length us, event | category | flops | bytes accessed | tf_op | source)
XLA Modules:
  0.0 34.2 jit_solution(10933918999671281476)
XLA Ops:
  0.0 33.4 %shard_map.217 = bf16[32,32,256]{2,1,0:T(8,128)(2,1)S(1)} custom-call(bf16[32,32,256]{2,1,0:T(8,128)(2,1)} %refs_0_.1, f32[1,256]{1,0:T(1,128)} %bitcast.14, f32[1,256]{1,0:T(1,128)} %bitcast.15, bf16[256,1024]{1,0:T(8,128)(2,1)} %refs_3_.1, f32[1,1024]{1,0:T(1,128)} %bitcast.11, f32[9,1024]{1,0:T(8,128)} %refs_5_.1, f32[1,1024]{1,0:T(1,128)} %bitcast.12, ...), custom_call_target="tpu_custom_call" | custom-call | tf_op jit(solution)/shard_map/pallas_call | solution.py:655
  33.4 0.8 %copy.25 = bf16[32,32,256]{2,1,0:T(8,128)(2,1)} copy(bf16[32,32,256]{2,1,0:T(8,128)(2,1)S(1)} %shard_map.217) | data formatting | bytes 1048576
